TPU v7x, 32 devices: a whole 2x2x4 slice. The times are simulated.
32 devices in a mesh: wide: 8 (over z, y), narrow: 4 (over x, core).
Axes of the slice: x: 2, y: 2, z: 4, core: 2. Of those that a mesh axis runs over, the one named last changes fastest.
Arguments:
- tokens: bfloat16 [32, 256, 1024], P(('wide', 'narrow')), may hold values from -6 to 6
- segment_ids: int32 [32, 256], P(('wide', 'narrow')), may hold values from 0 to 3, never falling along the last dimension, each value on 1 to 128 neighbouring positions
- routed_index: int32 [32, 32], P(('wide', 'narrow')), may hold values from 0 to 255, as said below
- out_grad: bfloat16 [32, 256, 1024], P(('wide', 'narrow')), may hold values from -6 to 6
- dense_attn_gain: bfloat16 [1024], P('wide'), may hold values from 0.5 to 1.5
- dense_qkv: bfloat16 [1024, 3072], P('wide'), may hold values from -0.1875 to 0.1875
- dense_proj: bfloat16 [1024, 1024], P('wide'), may hold values from -0.75 to 0.75
- dense_mlp_gain: bfloat16 [1024], P('wide'), may hold values from 0.5 to 1.5
- dense_up: bfloat16 [1024, 4096], P('wide'), may hold values from -0.1875 to 0.1875
- dense_down: bfloat16 [4096, 1024], P('wide'), may hold values from -0.09375 to 0.09375
- routed_attn_gain: bfloat16 [1024], P('wide'), may hold values from 0.5 to 1.5
- routed_qkv: bfloat16 [1024, 3072], P('wide'), may hold values from -0.1875 to 0.1875
- routed_proj: bfloat16 [1024, 1024], P('wide'), may hold values from -0.75 to 0.75
- routed_mlp_gain: bfloat16 [1024], P('wide'), may hold values from 0.5 to 1.5
- routed_up: bfloat16 [1024, 4096], P('wide'), may hold values from -0.1875 to 0.1875
- routed_down: bfloat16 [4096, 1024], P('wide'), may hold values from -0.09375 to 0.09375
- router_vector: bfloat16 [1024], replicated, may hold values from -0.1875 to 0.1875
Outputs:
- result: bfloat16 [32, 256, 1024], P(('wide', 'narrow'))
- input_grad: bfloat16 [32, 256, 1024], P(('wide', 'narrow'))
- grad_dense_attn_gain: float32 [1024], P('wide')
- grad_dense_qkv: float32 [1024, 3072], P('wide')
- grad_dense_proj: float32 [1024, 1024], P('wide')
- grad_dense_mlp_gain: float32 [1024], P('wide')
- grad_dense_up: float32 [1024, 4096], P('wide')
- grad_dense_down: float32 [4096, 1024], P('wide')
- grad_routed_attn_gain: float32 [1024], P('wide')
- grad_routed_qkv: float32 [1024, 3072], P('wide')
- grad_routed_proj: float32 [1024, 1024], P('wide')
- grad_routed_mlp_gain: float32 [1024], P('wide')
- grad_routed_up: float32 [1024, 4096], P('wide')
- grad_routed_down: float32 [4096, 1024], P('wide')
- router_grad: float32 [1024], replicated
Inputs may be any that keep to these rules, and one draw needn't show every extreme that they name: `routed_index`: each row holds 32 distinct positions of its sequence in increasing order.
All inputs are finite; a program needn't handle non-finite values.
Results may differ from a plain program's by a relative error of at most 0.022.
Values may be sent and summed in bfloat16 or wider, within the bound.
No kernel may reach another device: no remote copies, remote signals or barrier semaphores. Data moves between devices by JAX's collectives and lax.ppermute only.
A program may use at most 256 MiB of HBM per device.

v0:
```python
import jax
import jax.numpy as jnp
from jax import lax
from jax.sharding import PartitionSpec as P

HEADS = 16
EPS = 1e-06
NEG = -1e30
HIGH = lax.Precision.HIGHEST
GROUP_HEADS = 4


def rms_norm(values, gain):
    return values * lax.rsqrt(jnp.mean(values * values, -1, keepdims=True) + EPS) * gain


def gelu_tanh(values):
    return jax.nn.gelu(values, approximate=True)


def row_dot(left, right):
    return jnp.dot(left, right, preferred_element_type=jnp.float32)


def cross_dot(left, right):
    return lax.dot_general(
        left, right, (((0,), (0,)), ((), ())), preferred_element_type=jnp.float32
    )


def back_dot(left, right):
    return lax.dot_general(
        left, right, (((1,), (1,)), ((), ())), preferred_element_type=jnp.float32
    )


def block_mask(query_pos, query_seg, key_pos, key_seg):
    return (key_pos[None, :] <= query_pos[:, None]) & (key_seg[None, :] == query_seg[:, None])


def attend_forward(queries, key_rows, val_rows, positions, segments):
    row_count, head_count, head_width = queries.shape
    block_rows = min(512, row_count)
    block_count = row_count // block_rows
    score_scale = head_width ** (-0.5)
    group_size = min(GROUP_HEADS, head_count)

    def one_block(packed):
        query_blk, query_pos, query_seg = packed
        allowed = block_mask(query_pos, query_seg, positions, segments)[None]
        outputs = []
        logsums = []
        for head_start in range(0, head_count, group_size):
            head_slice = slice(head_start, head_start + group_size)
            scores = (
                jnp.einsum(
                    "qhd,khd->hqk",
                    query_blk[:, head_slice],
                    key_rows[:, head_slice],
                    preferred_element_type=jnp.float32,
                )
                * score_scale
            )
            scores = jnp.where(allowed, scores, NEG)
            highest = jnp.max(scores, -1, keepdims=True)
            lifted = jnp.exp(scores - highest)
            summed = jnp.sum(lifted, -1, keepdims=True)
            attn_prob = (lifted / summed).astype(jnp.bfloat16)
            outputs.append(
                jnp.einsum(
                    "hqk,khd->qhd",
                    attn_prob,
                    val_rows[:, head_slice],
                    preferred_element_type=jnp.float32,
                )
            )
            logsums.append((highest + jnp.log(summed))[:, :, 0])
        return (jnp.concatenate(outputs, 1), jnp.concatenate(logsums, 0))

    stacked = (
        queries.reshape(block_count, block_rows, head_count, head_width),
        positions.reshape(block_count, block_rows),
        segments.reshape(block_count, block_rows),
    )
    output, logsum = lax.map(one_block, stacked)
    return (output.reshape(row_count, head_count, head_width), logsum)


def attend_backward(queries, key_rows, val_rows, positions, segments, logsum, output_grad):
    row_count, head_count, head_width = queries.shape
    block_rows = min(512, row_count)
    block_count = row_count // block_rows
    score_scale = head_width ** (-0.5)
    group_size = min(GROUP_HEADS, head_count)

    def one_block(carry, packed):
        key_grad, val_grad = carry
        query_blk, query_pos, query_seg, logsum_blk, grad_blk = packed
        allowed = block_mask(query_pos, query_seg, positions, segments)[None]
        query_parts = []
        key_parts = []
        val_parts = []
        for head_start in range(0, head_count, group_size):
            head_slice = slice(head_start, head_start + group_size)
            scores = (
                jnp.einsum(
                    "qhd,khd->hqk",
                    query_blk[:, head_slice],
                    key_rows[:, head_slice],
                    preferred_element_type=jnp.float32,
                )
                * score_scale
            )
            scores = jnp.where(allowed, scores, NEG)
            attn_prob = jnp.exp(scores - logsum_blk[head_slice][:, :, None])
            prob_grad = jnp.einsum(
                "qhd,khd->hqk",
                grad_blk[:, head_slice],
                val_rows[:, head_slice],
                preferred_element_type=jnp.float32,
            )
            row_inner = jnp.sum(attn_prob * prob_grad, -1, keepdims=True)
            score_grad = (attn_prob * (prob_grad - row_inner)).astype(jnp.bfloat16)
            query_parts.append(
                jnp.einsum(
                    "hqk,khd->qhd",
                    score_grad,
                    key_rows[:, head_slice],
                    preferred_element_type=jnp.float32,
                )
                * score_scale
            )
            key_parts.append(
                jnp.einsum(
                    "hqk,qhd->khd",
                    score_grad,
                    query_blk[:, head_slice],
                    preferred_element_type=jnp.float32,
                )
                * score_scale
            )
            val_parts.append(
                jnp.einsum(
                    "hqk,qhd->khd",
                    attn_prob.astype(jnp.bfloat16),
                    grad_blk[:, head_slice],
                    preferred_element_type=jnp.float32,
                )
            )
        updated = (
            key_grad + jnp.concatenate(key_parts, 1),
            val_grad + jnp.concatenate(val_parts, 1),
        )
        return (updated, jnp.concatenate(query_parts, 1))

    zero_grad = jnp.zeros(key_rows.shape, jnp.float32)
    stacked = (
        queries.reshape(block_count, block_rows, head_count, head_width),
        positions.reshape(block_count, block_rows),
        segments.reshape(block_count, block_rows),
        logsum,
        output_grad.reshape(block_count, block_rows, head_count, head_width),
    )
    (key_grad, val_grad), query_grad = lax.scan(one_block, (zero_grad, zero_grad), stacked)
    return (query_grad.reshape(row_count, head_count, head_width), key_grad, val_grad)


def attend_layer(inputs, gain, mixing, project, positions, segments):
    row_count, model_width = inputs.shape
    normed, norm_back = jax.vjp(rms_norm, inputs, gain)
    normed_low = normed.astype(jnp.bfloat16)
    combined = row_dot(normed_low, mixing).astype(jnp.bfloat16)
    parts = combined.reshape(row_count, 3, HEADS, model_width // HEADS)
    queries = parts[:, 0]
    key_rows = parts[:, 1]
    val_rows = parts[:, 2]
    output, logsum = attend_forward(queries, key_rows, val_rows, positions, segments)
    output_low = output.reshape(row_count, model_width).astype(jnp.bfloat16)
    branch = row_dot(output_low, project)
    return (branch, (norm_back, normed_low, queries, key_rows, val_rows, logsum, output_low))


def attend_layer_back(branch_grad, kept, mixing, project, positions, segments):
    norm_back, normed_low, queries, key_rows, val_rows, logsum, output_low = kept
    row_count = output_low.shape[0]
    grad_low = branch_grad.astype(jnp.bfloat16)
    project_grad = cross_dot(output_low, grad_low)
    output_grad = back_dot(grad_low, project).astype(jnp.bfloat16)
    query_grad, key_grad, val_grad = attend_backward(
        queries, key_rows, val_rows, positions, segments, logsum, output_grad.reshape(queries.shape)
    )
    combined_grad = (
        jnp.stack([query_grad, key_grad, val_grad], 1).reshape(row_count, -1).astype(jnp.bfloat16)
    )
    mixing_grad = cross_dot(normed_low, combined_grad)
    input_grad, gain_grad = norm_back(back_dot(combined_grad, mixing))
    return (input_grad, gain_grad, mixing_grad, project_grad)


def feed_layer(inputs, gain, upward, downward):
    normed, norm_back = jax.vjp(rms_norm, inputs, gain)
    normed_low = normed.astype(jnp.bfloat16)
    hidden_pre = row_dot(normed_low, upward)
    active, gelu_back = jax.vjp(gelu_tanh, hidden_pre)
    active_low = active.astype(jnp.bfloat16)
    return (row_dot(active_low, downward), (norm_back, normed_low, gelu_back, active_low))


def feed_layer_back(branch_grad, kept, upward, downward):
    norm_back, normed_low, gelu_back, active_low = kept
    grad_low = branch_grad.astype(jnp.bfloat16)
    down_grad = cross_dot(active_low, grad_low)
    active_grad = back_dot(grad_low, downward)
    pre_grad = gelu_back(active_grad)[0].astype(jnp.bfloat16)
    up_grad = cross_dot(normed_low, pre_grad)
    input_grad, gain_grad = norm_back(back_dot(pre_grad, upward))
    return (input_grad, gain_grad, up_grad, down_grad)


def fetch_weights(weights):
    attn_gain, mixing, project, feed_gain, upward, downward = weights
    return (
        lax.all_gather(attn_gain, "wide", axis=0, tiled=True),
        lax.all_gather(mixing, "wide", axis=0, tiled=True),
        lax.all_gather(project, "wide", axis=0, tiled=True),
        lax.all_gather(feed_gain, "wide", axis=0, tiled=True),
        lax.all_gather(upward, "wide", axis=0, tiled=True),
        lax.all_gather(downward, "wide", axis=0, tiled=True),
    )


def reduce_grads(grads):
    attn_gain, mixing, project, feed_gain, upward, downward = grads
    shares = (
        lax.psum_scatter(
            attn_gain.astype(jnp.bfloat16), "wide", scatter_dimension=0, tiled=True
        ).astype(jnp.float32),
        lax.psum_scatter(
            mixing.astype(jnp.bfloat16), "wide", scatter_dimension=0, tiled=True
        ).astype(jnp.float32),
        lax.psum_scatter(
            project.astype(jnp.bfloat16), "wide", scatter_dimension=0, tiled=True
        ).astype(jnp.float32),
        lax.psum_scatter(
            feed_gain.astype(jnp.bfloat16), "wide", scatter_dimension=0, tiled=True
        ).astype(jnp.float32),
        lax.psum_scatter(
            upward.astype(jnp.bfloat16), "wide", scatter_dimension=0, tiled=True
        ).astype(jnp.float32),
        lax.psum_scatter(
            downward.astype(jnp.bfloat16), "wide", scatter_dimension=0, tiled=True
        ).astype(jnp.float32),
    )
    return (
        lax.psum(shares[0].astype(jnp.bfloat16), "narrow").astype(jnp.float32),
        lax.psum(shares[1].astype(jnp.bfloat16), "narrow").astype(jnp.float32),
        lax.psum(shares[2].astype(jnp.bfloat16), "narrow").astype(jnp.float32),
        lax.psum(shares[3].astype(jnp.bfloat16), "narrow").astype(jnp.float32),
        lax.psum(shares[4].astype(jnp.bfloat16), "narrow").astype(jnp.float32),
        lax.psum(shares[5].astype(jnp.bfloat16), "narrow").astype(jnp.float32),
    )


def per_device(
    tokens,
    segment_ids,
    routed_index,
    out_grad,
    dense_attn_gain,
    dense_qkv,
    dense_proj,
    dense_mlp_gain,
    dense_up,
    dense_down,
    routed_attn_gain,
    routed_qkv,
    routed_proj,
    routed_mlp_gain,
    routed_up,
    routed_down,
    router_vector,
):
    inputs = tokens[0].astype(jnp.float32)
    segments = segment_ids[0]
    chosen = routed_index[0]
    positions = jnp.arange(inputs.shape[0], dtype=jnp.int32)
    dense_full = fetch_weights(
        (dense_attn_gain, dense_qkv, dense_proj, dense_mlp_gain, dense_up, dense_down)
    )
    routed_full = fetch_weights(
        (routed_attn_gain, routed_qkv, routed_proj, routed_mlp_gain, routed_up, routed_down)
    )
    dense_att, dense_kept_att = attend_layer(
        inputs, dense_full[0].astype(jnp.float32), dense_full[1], dense_full[2], positions, segments
    )
    hidden = inputs + dense_att
    dense_ffn, dense_kept_ffn = feed_layer(
        hidden, dense_full[3].astype(jnp.float32), dense_full[4], dense_full[5]
    )
    middle = hidden + dense_ffn
    selected = jnp.take(middle, chosen, axis=0)
    chosen_seg = jnp.take(segments, chosen)
    route_vec = router_vector.astype(jnp.float32)
    rate = jax.nn.sigmoid(jnp.dot(selected, route_vec, precision=HIGH))
    routed_att, routed_kept_att = attend_layer(
        selected,
        routed_full[0].astype(jnp.float32),
        routed_full[1],
        routed_full[2],
        chosen,
        chosen_seg,
    )
    after_att = selected + routed_att
    routed_ffn, routed_kept_ffn = feed_layer(
        after_att, routed_full[3].astype(jnp.float32), routed_full[4], routed_full[5]
    )
    change = routed_att + routed_ffn
    result = middle.at[chosen].add(rate[:, None] * change)
    result_grad = out_grad[0].astype(jnp.float32)
    picked_grad = jnp.take(result_grad, chosen, axis=0)
    rate_grad = jnp.sum(picked_grad * change, -1)
    change_grad = rate[:, None] * picked_grad
    logit_grad = rate_grad * rate * (1.0 - rate)
    after_grad, routed_feed_gain_grad, routed_up_grad, routed_down_grad = feed_layer_back(
        change_grad, routed_kept_ffn, routed_full[4], routed_full[5]
    )
    att_in_grad, routed_attn_gain_grad, routed_qkv_grad, routed_proj_grad = attend_layer_back(
        change_grad + after_grad,
        routed_kept_att,
        routed_full[1],
        routed_full[2],
        chosen,
        chosen_seg,
    )
    selected_grad = after_grad + att_in_grad + logit_grad[:, None] * route_vec[None, :]
    router_local = jnp.dot(logit_grad, selected, precision=HIGH)
    routed_grads = reduce_grads(
        (
            routed_attn_gain_grad,
            routed_qkv_grad,
            routed_proj_grad,
            routed_feed_gain_grad,
            routed_up_grad,
            routed_down_grad,
        )
    )
    router_total = lax.psum(router_local, ("wide", "narrow"))
    middle_grad = result_grad.at[chosen].add(selected_grad)
    hidden_in_grad, dense_feed_gain_grad, dense_up_grad, dense_down_grad = feed_layer_back(
        middle_grad, dense_kept_ffn, dense_full[4], dense_full[5]
    )
    hidden_grad = middle_grad + hidden_in_grad
    input_part, dense_attn_gain_grad, dense_qkv_grad, dense_proj_grad = attend_layer_back(
        hidden_grad, dense_kept_att, dense_full[1], dense_full[2], positions, segments
    )
    input_total = hidden_grad + input_part
    dense_grads = reduce_grads(
        (
            dense_attn_gain_grad,
            dense_qkv_grad,
            dense_proj_grad,
            dense_feed_gain_grad,
            dense_up_grad,
            dense_down_grad,
        )
    )
    return (
        result.astype(jnp.bfloat16)[None],
        input_total.astype(jnp.bfloat16)[None],
        dense_grads[0],
        dense_grads[1],
        dense_grads[2],
        dense_grads[3],
        dense_grads[4],
        dense_grads[5],
        routed_grads[0],
        routed_grads[1],
        routed_grads[2],
        routed_grads[3],
        routed_grads[4],
        routed_grads[5],
        router_total,
    )


def solution(mesh):
    return jax.shard_map(
        per_device,
        mesh=mesh,
        in_specs=(
            P(("wide", "narrow"), None, None),
            P(("wide", "narrow"), None),
            P(("wide", "narrow"), None),
            P(("wide", "narrow"), None, None),
            P("wide"),
            P("wide", None),
            P("wide", None),
            P("wide"),
            P("wide", None),
            P("wide", None),
            P("wide"),
            P("wide", None),
            P("wide", None),
            P("wide"),
            P("wide", None),
            P("wide", None),
            P(),
        ),
        out_specs=(
            P(("wide", "narrow"), None, None),
            P(("wide", "narrow"), None, None),
            P("wide"),
            P("wide", None),
            P("wide", None),
            P("wide"),
            P("wide", None),
            P("wide", None),
            P("wide"),
            P("wide", None),
            P("wide", None),
            P("wide"),
            P("wide", None),
            P("wide", None),
            P(),
        ),
        check_vma=False,
    )
```

profile of v0, /device:TPU:0, one launch (start us, length us, event | category | flops | bytes accessed | tf_op | source)
XLA Modules:
  0.0 1981.9 jit_solution(2973243669548970490)
XLA Ops:
  14.0 22.8 %all-gather = bf16[8,1,128]{2,1,0:T(2,128)(2,1)S(1)} all-gather(bf16[1,1,128]{2,1,0:T(2,128)(2,1)S(1)} %bitcast.332), channel_id=1, replica_groups=mesh['wide'=8,'narrow'=4] {'wide'}, dimensions={0}, use_global_device_ids=true | all-gather | bytes 2304 | tf_op jit(solution)/shard_map/all_gather | solution.py:223
  36.8 16.9 all-gather.1
  53.7 18.9 all-gather.2
  72.5 16.9 all-gather.3
  92.5 19.4 all-gather.13.cloned.1.call-done
  124.2 37.1 %all-gather.15.cloned.1.call-done = bf16[1024,1024]{1,0:T(8,128)(2,1)} async-done(((bf16[128,1024]{1,0:T(8,128)(2,1)}), bf16[1024,1024]{1,0:T(8,128)(2,1)}) %all-gather.15.cloned.1.call-update) | async-done | bytes 2097168 | tf_op jit(solution)/shard_map/all_gather | solution.py:225
  163.8 122.7 %all-gather.17.cloned.1.call-done = bf16[1024,4096]{1,0:T(8,128)(2,1)} async-done(((bf16[128,4096]{1,0:T(8,128)(2,1)}), bf16[1024,4096]{1,0:T(8,128)(2,1)}) %all-gather.17.cloned.1.call-update) | async-done | bytes 8388624 | tf_op jit(solution)/shard_map/all_gather | solution.py:227
  294.3 116.9 %all-gather.19.cloned.1.call-done = bf16[4096,1024]{1,0:T(8,128)(2,1)} async-done(((bf16[512,1024]{1,0:T(8,128)(2,1)}), bf16[4096,1024]{1,0:T(8,128)(2,1)}) %all-gather.19.cloned.1.call-update) | async-done | bytes 8388624 | tf_op jit(solution)/shard_map/all_gather | solution.py:228
  419.5 90.7 %all-gather.21.cloned.1.call-done = bf16[1024,3072]{1,0:T(8,128)(2,1)} async-done(((bf16[128,3072]{1,0:T(8,128)(2,1)}), bf16[1024,3072]{1,0:T(8,128)(2,1)}) %all-gather.21.cloned.1.call-update) | async-done | bytes 6291472 | tf_op jit(solution)/shard_map/all_gather | solution.py:224
  516.6 43.1 %all-gather.23.cloned.1.call-done = bf16[1024,1024]{1,0:T(8,128)(2,1)} async-done(((bf16[128,1024]{1,0:T(8,128)(2,1)}), bf16[1024,1024]{1,0:T(8,128)(2,1)}) %all-gather.23.cloned.1.call-update) | async-done | bytes 2097168 | tf_op jit(solution)/shard_map/all_gather | solution.py:225
  562.8 122.0 %all-gather.25.cloned.1.call-done = bf16[1024,4096]{1,0:T(8,128)(2,1)} async-done(((bf16[128,4096]{1,0:T(8,128)(2,1)}), bf16[1024,4096]{1,0:T(8,128)(2,1)}) %all-gather.25.cloned.1.call-update) | async-done | bytes 8388624 | tf_op jit(solution)/shard_map/all_gather | solution.py:227
  690.0 119.6 %all-gather.27.cloned.1.call-done = bf16[4096,1024]{1,0:T(8,128)(2,1)} async-done(((bf16[512,1024]{1,0:T(8,128)(2,1)}), bf16[4096,1024]{1,0:T(8,128)(2,1)}) %all-gather.27.cloned.1.call-update) | async-done | bytes 8388624 | tf_op jit(solution)/shard_map/all_gather | solution.py:228
  838.4 9.3 fusion.6
  907.4 8.4 convolution_convert_fusion.2
  929.3 66.9 %reduce-scatter.19.cloned.1.call-done = bf16[128,1024]{1,0:T(8,128)(2,1)} async-done(((bf16[1024,1024]{1,0:T(8,128)(2,1)}), bf16[128,1024]{1,0:T(8,128)(2,1)}) %reduce-scatter.19.cloned.1.call-update) | async-done | bytes 262160 | tf_op jit(solution)/shard_map/reduce_scatter | solution.py:241
  996.3 120.7 %reduce-scatter.9.cloned.1.call-done = bf16[128,3072]{1,0:T(8,128)(2,1)} async-done(((bf16[1024,3072]{1,0:T(8,128)(2,1)}), bf16[128,3072]{1,0:T(8,128)(2,1)}) %reduce-scatter.9.cloned.1.call-update) | async-done | bytes 786448 | tf_op jit(solution)/shard_map/reduce_scatter | solution.py:238
  1116.9 120.8 %reduce-scatter.17.cloned.1.call-done = bf16[128,3072]{1,0:T(8,128)(2,1)} async-done(((bf16[1024,3072]{1,0:T(8,128)(2,1)}), bf16[128,3072]{1,0:T(8,128)(2,1)}) %reduce-scatter.17.cloned.1.call-update) | async-done | bytes 786448 | tf_op jit(solution)/shard_map/reduce_scatter | solution.py:238
  1237.7 150.3 %reduce-scatter.13.cloned.1.call-done = bf16[128,4096]{1,0:T(8,128)(2,1)} async-done(((bf16[1024,4096]{1,0:T(8,128)(2,1)}), bf16[128,4096]{1,0:T(8,128)(2,1)}) %reduce-scatter.13.cloned.1.call-update) | async-done | bytes 1048592 | tf_op jit(solution)/shard_map/reduce_scatter | solution.py:247
  1388.0 150.1 %reduce-scatter.15.cloned.1.call-done = bf16[512,1024]{1,0:T(8,128)(2,1)} async-done(((bf16[4096,1024]{1,0:T(8,128)(2,1)}), bf16[512,1024]{1,0:T(8,128)(2,1)}) %reduce-scatter.15.cloned.1.call-update) | async-done | bytes 1048592 | tf_op jit(solution)/shard_map/reduce_scatter | solution.py:250
  1538.1 150.1 %reduce-scatter.21.cloned.1.call-done = bf16[128,4096]{1,0:T(8,128)(2,1)} async-done(((bf16[1024,4096]{1,0:T(8,128)(2,1)}), bf16[128,4096]{1,0:T(8,128)(2,1)}) %reduce-scatter.21.cloned.1.call-update) | async-done | bytes 1048592 | tf_op jit(solution)/shard_map/reduce_scatter | solution.py:247
  1688.2 150.1 %reduce-scatter.23.cloned.1.call-done = bf16[512,1024]{1,0:T(8,128)(2,1)} async-done(((bf16[4096,1024]{1,0:T(8,128)(2,1)}), bf16[512,1024]{1,0:T(8,128)(2,1)}) %reduce-scatter.23.cloned.1.call-update) | async-done | bytes 1048592 | tf_op jit(solution)/shard_map/reduce_scatter | solution.py:250
  1847.2 19.7 all-reduce.4
  1876.0 37.8 %psum.103 = f32[1024]{0:T(1024)} all-reduce(f32[1024]{0:T(1024)S(1)} %bitcast.330), channel_id=1, replica_groups=mesh['wide'=8,'narrow'=4] {'wide','narrow'}, use_global_device_ids=true, to_apply=%region_63.65 | all-reduce | flops 1024 | bytes 8192 | tf_op jit(solution)/shard_map/psum | solution.py:347
  1917.1 44.0 %all-reduce.9.cloned.1.call-done = (bf16[128,3072]{1,0:T(8,128)(2,1)}, bf16[128,1024]{1,0:T(8,128)(2,1)}, bf16[128,4096]{1,0:T(8,128)(2,1)}, bf16[512,1024]{1,0:...) async-done(((bf16[128,3072]{1,0:T(8,128)(2,1)}, bf16[128,1024]{1,0:T(8,128)(2,1)}, ...) | async-done | bytes 6291472 | tf_op jit(solution)/shard_map/psum | solution.py:256
  (423 shorter events, 190.2 us)
Async XLA Ops:
  7.3 104.6 %all-gather.13.cloned.1.call-start = ((), (), s32[]{:S(2)}) async-start(), calls=%async_computation.8 | async-start | bytes 7077888 | tf_op jit(solution)/shard_map/all_gather | solution.py:224
  8.0 153.4 %all-gather.15.cloned.1.call-start = ((), (), s32[]{:S(2)}) async-start(), calls=%async_computation.9 | async-start | bytes 2359296 | tf_op jit(solution)/shard_map/all_gather | solution.py:225
  8.8 277.8 %all-gather.17.cloned.1.call-start = ((), (), s32[]{:S(2)}) async-start(), calls=%async_computation.10 | async-start | bytes 9437184 | tf_op jit(solution)/shard_map/all_gather | solution.py:227
  9.5 401.7 %all-gather.19.cloned.1.call-start = ((), (), s32[]{:S(2)}) async-start(), calls=%async_computation.11 | async-start | bytes 9437184 | tf_op jit(solution)/shard_map/all_gather | solution.py:228
  10.1 500.1 %all-gather.21.cloned.1.call-start = ((), (), s32[]{:S(2)}) async-start(), calls=%async_computation.12 | async-start | bytes 7077888 | tf_op jit(solution)/shard_map/all_gather | solution.py:224
  10.7 549.0 %all-gather.23.cloned.1.call-start = ((), (), s32[]{:S(2)}) async-start(), calls=%async_computation.13 | async-start | bytes 2359296 | tf_op jit(solution)/shard_map/all_gather | solution.py:225
  11.2 673.6 %all-gather.25.cloned.1.call-start = ((), (), s32[]{:S(2)}) async-start(), calls=%async_computation.14 | async-start | bytes 9437184 | tf_op jit(solution)/shard_map/all_gather | solution.py:227
  12.0 797.7 %all-gather.27.cloned.1.call-start = ((), (), s32[]{:S(2)}) async-start(), calls=%async_computation.15 | async-start | bytes 9437184 | tf_op jit(solution)/shard_map/all_gather | solution.py:228
  12.7 916.6 %reduce-scatter.11.cloned.1.call-start = ((), (), s32[]{:S(2)}) async-start(), calls=%async_computation.17 | async-start | bytes 2359296 | tf_op jit(solution)/shard_map/reduce_scatter | solution.py:241
  90.7 419.5 %copy-start.45 = (pred[32]{0:T(512)(128)(4,1)}, pred[32]{0:T(512)(128)(4,1)S(1)}, u32[]{:S(2)}) copy-start(pred[32]{0:T(512)(128)(4,1)S(1)} %get-tuple-element.170) | copy-start | bytes 100
  562.5 256.6 %copy-start.57 = (f32[32]{0:T(128)}, f32[32]{0:T(128)S(1)}, u32[]{:S(2)}) copy-start(f32[32]{0:T(128)S(1)} %fusion.202) | copy-start | bytes 388
  562.8 256.3 %copy-start.79 = (f32[32]{0:T(128)}, f32[32]{0:T(128)S(1)}, u32[]{:S(2)}) copy-start(f32[32]{0:T(128)S(1)} %fusion.60) | copy-start | bytes 388
  858.2 138.1 %reduce-scatter.19.cloned.1.call-start = ((), (), s32[]{:S(2)}) async-start(), calls=%async_computation.21 | async-start | bytes 2359296 | tf_op jit(solution)/shard_map/reduce_scatter | solution.py:241
  878.8 238.1 %reduce-scatter.9.cloned.1.call-start = ((), (), s32[]{:S(2)}) async-start(), calls=%async_computation.16 | async-start | bytes 7077888 | tf_op jit(solution)/shard_map/reduce_scatter | solution.py:238
  892.8 344.9 %reduce-scatter.17.cloned.1.call-start = ((), (), s32[]{:S(2)}) async-start(), calls=%async_computation.20 | async-start | bytes 7077888 | tf_op jit(solution)/shard_map/reduce_scatter | solution.py:238
  898.2 489.9 %reduce-scatter.13.cloned.1.call-start = ((), (), s32[]{:S(2)}) async-start(), calls=%async_computation.18 | async-start | bytes 9437184 | tf_op jit(solution)/shard_map/reduce_scatter | solution.py:247
  906.2 631.9 %reduce-scatter.15.cloned.1.call-start = ((), (), s32[]{:S(2)}) async-start(), calls=%async_computation.19 | async-start | bytes 9437184 | tf_op jit(solution)/shard_map/reduce_scatter | solution.py:250
  915.9 772.3 %reduce-scatter.21.cloned.1.call-start = ((), (), s32[]{:S(2)}) async-start(), calls=%async_computation.22 | async-start | bytes 9437184 | tf_op jit(solution)/shard_map/reduce_scatter | solution.py:247
  922.5 915.7 %reduce-scatter.23.cloned.1.call-start = ((), (), s32[]{:S(2)}) async-start(), calls=%async_computation.23 | async-start | bytes 9437184 | tf_op jit(solution)/shard_map/reduce_scatter | solution.py:250
  929.2 909.0 %copy-start.105 = (u32[32]{0:T(128)S(1)}, u32[32]{0:T(128)}, u32[]{:S(2)}) copy-start(u32[32]{0:T(128)} %constant.160) | copy-start | bytes 388
  929.2 910.3 %copy-start.24 = (f32[256,1024]{1,0:T(8,128)S(1)}, f32[256,1024]{1,0:T(8,128)}, u32[]{:S(2)}) copy-start(f32[256,1024]{1,0:T(8,128)} %copy-done.23) | copy-start | bytes 3145732
  929.2 910.3 %copy-start.32 = (f32[32,1024]{1,0:T(8,128)S(1)}, f32[32,1024]{1,0:T(8,128)}, u32[]{:S(2)}) copy-start(f32[32,1024]{1,0:T(8,128)} %copy-done.31) | copy-start | bytes 393220
  929.2 911.7 %copy-start.61 = (f32[256]{0:T(256)S(1)}, f32[256]{0:T(256)}, u32[]{:S(2)}) copy-start(f32[256]{0:T(256)} %copy-done.59) | copy-start | bytes 3076
  929.3 1031.9 %all-reduce.9.cloned.1.call-start = ((), (), s32[]{:S(2)}) async-start(), calls=%async_computation.24 | async-start | bytes 12582912 | tf_op jit(solution)/shard_map/psum | solution.py:256
  (101 other events, 2080.3 us)
Sparse Core Ops, SparseCore 0:
  10.3 101.5 all-gather.12
  114.0 47.3 all-gather.14
  163.5 122.9 all-gather.16
  288.5 122.6 all-gather.18
  413.2 96.8 all-gather.20
  512.1 47.4 all-gather.22
  561.8 122.9 all-gather.24
  687.0 122.6 all-gather.26
  858.3 66.6 reduce-scatter.10
  928.9 67.2 reduce-scatter.18
  999.8 117.0 reduce-scatter.8
  1120.4 117.2 reduce-scatter.16
  1241.3 146.6 reduce-scatter.12
  1391.5 146.5 reduce-scatter.14
  1541.6 146.5 reduce-scatter.20
  1691.6 146.5 reduce-scatter.22
  1840.9 120.1 all-reduce.8
where the time goes:
time: 1990 us; the launch traced here: 1980 us
  waiting for transfers between devices  1630 us (82%)
  matrix products  143 us (7%)
  blocking collectives  139 us (7%)
  other arithmetic  35.4 us (2%)
    reduce_scatter x2, waiting for transfers between devices, reduce_grads(): lax.psum_scatter(upward.astype(jnp.bfloat16), 'wide', scatter_dimension=0...  300 us
    reduce_scatter x2, waiting for transfers between devices, reduce_grads(): lax.psum_scatter(downward.astype(jnp.bfloat16), 'wide', scatter_dimension...  300 us
    all_gather x2, waiting for transfers between devices, fetch_weights(): lax.all_gather(upward, 'wide', axis=0, tiled=True)  245 us
    reduce_scatter x2, waiting for transfers between devices, reduce_grads(): lax.psum_scatter(mixing.astype(jnp.bfloat16), 'wide', scatter_dimension=0...  241 us
    all_gather x2, waiting for transfers between devices, fetch_weights(): lax.all_gather(downward, 'wide', axis=0, tiled=True)  237 us
    all_gather x2, waiting for transfers between devices, fetch_weights(): lax.all_gather(mixing, 'wide', axis=0, tiled=True)  110 us
    all_gather x2, waiting for transfers between devices, fetch_weights(): lax.all_gather(project, 'wide', axis=0, tiled=True)  80.2 us
    reduce_scatter x2, waiting for transfers between devices, reduce_grads(): lax.psum_scatter(project.astype(jnp.bfloat16), 'wide', scatter_dimension=...  66.9 us
  transfers between devices with their start and end apart: 17, of which 16 were waited for; matrix products, arithmetic and copies ran while one was open for 6% of the time, Pallas kernels for 0%

commit v1 on v0

--- a/solution.py
+++ b/solution.py
@@ -8,6 +8,18 @@
 NEG = -1e30
 HIGH = lax.Precision.HIGHEST
 GROUP_HEADS = 4
+
+
+def doubled_up(x, axis, dim):
+    ways, here, hop = (lax.axis_size(axis), lax.axis_index(axis), x.shape[dim])
+    line, have = (x, 1)
+    while have < ways:
+        line = jnp.concatenate(
+            [line, lax.ppermute(line, axis, [(d, (d - have) % ways) for d in range(ways)])],
+            axis=dim,
+        )
+        have = 2 * have
+    return jnp.roll(line, here * hop, axis=dim)
 
 
 def rms_norm(values, gain):
@@ -225,7 +237,7 @@
         lax.all_gather(project, "wide", axis=0, tiled=True),
         lax.all_gather(feed_gain, "wide", axis=0, tiled=True),
         lax.all_gather(upward, "wide", axis=0, tiled=True),
-        lax.all_gather(downward, "wide", axis=0, tiled=True),
+        doubled_up(downward, "wide", 0),
     )
 
 

time: 1990 us -> 2230 us (1.12)
  blocking collectives: 139 us -> 407 us
  waiting for transfers between devices: 1630 us -> 1380 us
  starting transfers between devices: 1.06 us -> 104 us
  other arithmetic: 35.4 us -> 136 us
    all_gather x2 -> x0, waiting for transfers between devices: 237 us -> none  [fetch_weights(): lax.all_gather(downward, 'wide', axis=0, tiled=True)]
    ppermute x0 -> x6, waiting for transfers between devices: none -> 196 us  [doubled_up(): lax.ppermute(line, axis, [(d, (d - have) % ways) for d in range(ways)])]
    all_gather x2, blocking collectives: 33.8 us -> 214 us  [fetch_weights(): lax.all_gather(feed_gain, 'wide', axis=0, tiled=True)]
    all_gather x2, waiting for transfers between devices: 245 us -> 120 us  [fetch_weights(): lax.all_gather(upward, 'wide', axis=0, tiled=True)]
    ppermute x0 -> x6, starting transfers between devices: none -> 103 us  [doubled_up(): lax.ppermute(line, axis, [(d, (d - have) % ways) for d in range(ways)])]
    concatenate x0 -> x6, other arithmetic: none -> 92.3 us  [the longest x2 80.9 us: doubled_up(): return jnp.roll(line, here * hop, axis=dim)]
    all_gather x2, blocking collectives: 41.6 us -> 129 us  [fetch_weights(): lax.all_gather(attn_gain, 'wide', axis=0, tiled=True)]
    all_gather x2, waiting for transfers between devices: 80.2 us -> 38.5 us  [fetch_weights(): lax.all_gather(project, 'wide', axis=0, tiled=True)]
  transfers between devices with their start and end apart: 17 -> 21, of which waited for: 16 -> 14; matrix products, arithmetic and copies ran while one was open for 6% -> 10% of each run, Pallas kernels for 0% -> 0%
where the time goes in v1:
time: 2230 us; the launch traced here: 2220 us
  waiting for transfers between devices  1380 us (62%)
  blocking collectives  407 us (18%)
  matrix products  156 us (7%)
  other arithmetic  136 us (6%)
  starting transfers between devices  104 us (5%)
    reduce_scatter x2, waiting for transfers between devices, reduce_grads(): lax.psum_scatter(upward.astype(jnp.bfloat16), 'wide', scatter_dimension=0...  301 us
    reduce_scatter x2, waiting for transfers between devices, reduce_grads(): lax.psum_scatter(downward.astype(jnp.bfloat16), 'wide', scatter_dimension...  300 us
    reduce_scatter x2, waiting for transfers between devices, reduce_grads(): lax.psum_scatter(mixing.astype(jnp.bfloat16), 'wide', scatter_dimension=0...  241 us
    all_gather x2, blocking collectives, fetch_weights(): lax.all_gather(feed_gain, 'wide', axis=0, tiled=True)  214 us
    ppermute x6, waiting for transfers between devices, doubled_up(): lax.ppermute(line, axis, [(d, (d - have) % ways) for d in range(ways)])  196 us
    all_gather x2, blocking collectives, fetch_weights(): lax.all_gather(attn_gain, 'wide', axis=0, tiled=True)  129 us
    all_gather x2, waiting for transfers between devices, fetch_weights(): lax.all_gather(upward, 'wide', axis=0, tiled=True)  120 us
    ppermute x6, starting transfers between devices, doubled_up(): lax.ppermute(line, axis, [(d, (d - have) % ways) for d in range(ways)])  103 us
  transfers between devices with their start and end apart: 21, of which 14 were waited for; matrix products, arithmetic and copies ran while one was open for 10% of the time, Pallas kernels for 0%

profile of v1, /device:TPU:0, one launch (start us, length us, event | category | flops | bytes accessed | tf_op | source)
XLA Modules:
  0.0 2221.3 jit_solution(17155097160085508881)
XLA Ops:
  16.1 40.6 %collective-permute-done = bf16[512,1024]{1,0:T(8,128)(2,1)S(1)} collective-permute-done((bf16[512,1024]{1,0:T(8,128)(2,1)}, bf16[512,1024]{1,0:T(8,128)(2,1)S(1)}, u32[]{:S(2)}, u32[]{:S(2)}) %collective-permute-start) | collective-permute-done | bytes 1048608 | tf_op jit(solution)/shard_map/ppermute | solution.py:18
  65.7 65.8 %collective-permute-done.3 = bf16[512,1024]{1,0:T(8,128)(2,1)S(1)} collective-permute-done((bf16[512,1024]{1,0:T(8,128)(2,1)S(1)}, bf16[512,1024]{1,0:T(8,128)(2,1)S(1)}, u32[]{:S(2)}, u32[]{:S(2)}) %collective-permute-start.3) | collective-permute-done | bytes 1048608 | tf_op jit(solution)/shard_map/ppermute | solution.py:18
  139.1 89.2 %collective-permute-done.4 = bf16[1024,1024]{1,0:T(8,128)(2,1)} collective-permute-done((bf16[1024,1024]{1,0:T(8,128)(2,1)}, bf16[1024,1024]{1,0:T(8,128)(2,1)}, u32[]{:S(2)}, u32[]{:S(2)}) %collective-permute-start.4) | collective-permute-done | bytes 2097184 | tf_op jit(solution)/shard_map/ppermute | solution.py:18
  231.9 89.6 %collective-permute-start.5 = (bf16[2048,1024]{1,0:T(8,128)(2,1)}, bf16[2048,1024]{1,0:T(8,128)(2,1)}, u32[]{:S(2)}, u32[]{:S(2)}) collective-permute-start(bf16[2048,1024]{1,0:T(8,128)(2,1)} %pad_maximum_fusion.1), channel_id=1, source_target_pairs={{0,16},{4,20},{8,24},{12,28},{16,0},{20,4},{24,8},{28,12},{1,17},{... | collective-permute-start | bytes 12582920 | tf_op jit(solution)/shard_map/ppermute | solution.py:18
  322.7 112.8 %all-gather = bf16[8,1,128]{2,1,0:T(2,128)(2,1)S(1)} all-gather(bf16[1,1,128]{2,1,0:T(2,128)(2,1)S(1)} %bitcast.330), channel_id=1, replica_groups=mesh['wide'=8,'narrow'=4] {'wide'}, dimensions={0}, use_global_device_ids=true | all-gather | bytes 2304 | tf_op jit(solution)/shard_map/all_gather | solution.py:235
  435.5 194.5 %all-gather.1 = bf16[8,1,128]{2,1,0:T(2,128)(2,1)S(1)} all-gather(bf16[1,1,128]{2,1,0:T(2,128)(2,1)S(1)} %bitcast.331), channel_id=1, replica_groups=mesh['wide'=8,'narrow'=4] {'wide'}, dimensions={0}, use_global_device_ids=true | all-gather | bytes 2304 | tf_op jit(solution)/shard_map/all_gather | solution.py:238
  630.0 16.3 all-gather.2
  646.3 19.4 all-gather.3
  668.2 35.1 %fusion.10 = bf16[4096,1024]{1,0:T(8,128)(2,1)} fusion(s32[]{:T(128)S(6)} %select_n.115, bf16[512,1024]{1,0:T(8,128)(2,1)S(1)} %copy-done.16, bf16[512,1024]{1,0:T(8,128)(2,1)} %copy-done.19, bf16[1024,1024]{1,0:T(8,128)(2,1)} %collective-permute-done.1, bf16[2048,1024]{1,0:T(8,128)(2,1)} %collective-permute-done.2), kind=kLoop, calls=%fused_computation.31 | loop fusion | flops 67108864 | bytes 16777220 | tf_op jit(solution)/shard_map/jit(_roll_dynamic)/concatenate | solution.py:22
  703.4 45.8 %fusion.3 = bf16[4096,1024]{1,0:T(8,128)(2,1)} fusion(s32[]{:T(128)S(6)} %select_n.115, bf16[512,1024]{1,0:T(8,128)(2,1)S(1)} %copy-done.18, bf16[512,1024]{1,0:T(8,128)(2,1)S(1)} %copy-done.22, bf16[1024,1024]{1,0:T(8,128)(2,1)} %collective-permute-done.4, bf16[2048,1024]{1,0:T(8,128)(2,1)} %collective-permute-done.5), kind=kLoop, calls=%fused_computation.24 | loop fusion | flops 67108864 | bytes 16777220 | tf_op jit(solution)/shard_map/jit(_roll_dynamic)/concatenate | solution.py:22
  779.2 75.0 %all-gather.17.cloned.1.call-done = bf16[1024,3072]{1,0:T(8,128)(2,1)} async-done(((bf16[128,3072]{1,0:T(8,128)(2,1)}), bf16[1024,3072]{1,0:T(8,128)(2,1)}) %all-gather.17.cloned.1.call-update) | async-done | bytes 6291472 | tf_op jit(solution)/shard_map/all_gather | solution.py:236
  865.0 38.5 %all-gather.19.cloned.1.call-done = bf16[1024,1024]{1,0:T(8,128)(2,1)} async-done(((bf16[128,1024]{1,0:T(8,128)(2,1)}), bf16[1024,1024]{1,0:T(8,128)(2,1)}) %all-gather.19.cloned.1.call-update) | async-done | bytes 2097168 | tf_op jit(solution)/shard_map/all_gather | solution.py:237
  909.0 119.5 %all-gather.21.cloned.1.call-done = bf16[1024,4096]{1,0:T(8,128)(2,1)} async-done(((bf16[128,4096]{1,0:T(8,128)(2,1)}), bf16[1024,4096]{1,0:T(8,128)(2,1)}) %all-gather.21.cloned.1.call-update) | async-done | bytes 8388624 | tf_op jit(solution)/shard_map/all_gather | solution.py:239
  1074.7 11.6 fusion.20
  1172.6 62.9 %reduce-scatter.19.cloned.1.call-done = bf16[128,1024]{1,0:T(8,128)(2,1)} async-done(((bf16[1024,1024]{1,0:T(8,128)(2,1)}), bf16[128,1024]{1,0:T(8,128)(2,1)}) %reduce-scatter.19.cloned.1.call-update) | async-done | bytes 262160 | tf_op jit(solution)/shard_map/reduce_scatter | solution.py:253
  1235.5 120.6 %reduce-scatter.9.cloned.1.call-done = bf16[128,3072]{1,0:T(8,128)(2,1)} async-done(((bf16[1024,3072]{1,0:T(8,128)(2,1)}), bf16[128,3072]{1,0:T(8,128)(2,1)}) %reduce-scatter.9.cloned.1.call-update) | async-done | bytes 786448 | tf_op jit(solution)/shard_map/reduce_scatter | solution.py:250
  1356.2 120.7 %reduce-scatter.17.cloned.1.call-done = bf16[128,3072]{1,0:T(8,128)(2,1)} async-done(((bf16[1024,3072]{1,0:T(8,128)(2,1)}), bf16[128,3072]{1,0:T(8,128)(2,1)}) %reduce-scatter.17.cloned.1.call-update) | async-done | bytes 786448 | tf_op jit(solution)/shard_map/reduce_scatter | solution.py:250
  1476.9 150.4 %reduce-scatter.13.cloned.1.call-done = bf16[128,4096]{1,0:T(8,128)(2,1)} async-done(((bf16[1024,4096]{1,0:T(8,128)(2,1)}), bf16[128,4096]{1,0:T(8,128)(2,1)}) %reduce-scatter.13.cloned.1.call-update) | async-done | bytes 1048592 | tf_op jit(solution)/shard_map/reduce_scatter | solution.py:259
  1627.3 150.1 %reduce-scatter.15.cloned.1.call-done = bf16[512,1024]{1,0:T(8,128)(2,1)} async-done(((bf16[4096,1024]{1,0:T(8,128)(2,1)}), bf16[512,1024]{1,0:T(8,128)(2,1)}) %reduce-scatter.15.cloned.1.call-update) | async-done | bytes 1048592 | tf_op jit(solution)/shard_map/reduce_scatter | solution.py:262
  1777.4 150.2 %reduce-scatter.21.cloned.1.call-done = bf16[128,4096]{1,0:T(8,128)(2,1)} async-done(((bf16[1024,4096]{1,0:T(8,128)(2,1)}), bf16[128,4096]{1,0:T(8,128)(2,1)}) %reduce-scatter.21.cloned.1.call-update) | async-done | bytes 1048592 | tf_op jit(solution)/shard_map/reduce_scatter | solution.py:259
  1927.6 150.1 %reduce-scatter.23.cloned.1.call-done = bf16[512,1024]{1,0:T(8,128)(2,1)} async-done(((bf16[4096,1024]{1,0:T(8,128)(2,1)}), bf16[512,1024]{1,0:T(8,128)(2,1)}) %reduce-scatter.23.cloned.1.call-update) | async-done | bytes 1048592 | tf_op jit(solution)/shard_map/reduce_scatter | solution.py:262
  2086.7 19.7 all-reduce.4
  2115.5 37.8 %psum.103 = f32[1024]{0:T(1024)} all-reduce(f32[1024]{0:T(1024)S(1)} %bitcast.328), channel_id=1, replica_groups=mesh['wide'=8,'narrow'=4] {'wide','narrow'}, use_global_device_ids=true, to_apply=%region_63.66 | all-reduce | flops 1024 | bytes 8192 | tf_op jit(solution)/shard_map/psum | solution.py:359
  2156.5 44.0 %all-reduce.9.cloned.1.call-done = (bf16[128,3072]{1,0:T(8,128)(2,1)}, bf16[128,1024]{1,0:T(8,128)(2,1)}, bf16[128,4096]{1,0:T(8,128)(2,1)}, bf16[512,1024]{1,0:...) async-done(((bf16[128,3072]{1,0:T(8,128)(2,1)}, bf16[128,1024]{1,0:T(8,128)(2,1)}, ...) | async-done | bytes 6291472 | tf_op jit(solution)/shard_map/psum | solution.py:268
  (408 shorter events, 244.8 us)
Async XLA Ops:
  7.2 742.0 %all-gather.11.cloned.1.call-start = ((), (), s32[]{:S(2)}) async-start(), calls=%async_computation.8 | async-start | bytes 7077888 | tf_op jit(solution)/shard_map/all_gather | solution.py:236
  7.9 753.6 %all-gather.13.cloned.1.call-start = ((), (), s32[]{:S(2)}) async-start(), calls=%async_computation.9 | async-start | bytes 2359296 | tf_op jit(solution)/shard_map/all_gather | solution.py:237
  8.7 755.5 %all-gather.15.cloned.1.call-start = ((), (), s32[]{:S(2)}) async-start(), calls=%async_computation.10 | async-start | bytes 9437184 | tf_op jit(solution)/shard_map/all_gather | solution.py:239
  9.4 844.8 %all-gather.17.cloned.1.call-start = ((), (), s32[]{:S(2)}) async-start(), calls=%async_computation.11 | async-start | bytes 7077888 | tf_op jit(solution)/shard_map/all_gather | solution.py:236
  10.0 893.5 %all-gather.19.cloned.1.call-start = ((), (), s32[]{:S(2)}) async-start(), calls=%async_computation.12 | async-start | bytes 2359296 | tf_op jit(solution)/shard_map/all_gather | solution.py:237
  10.0 46.6 %collective-permute-start = (bf16[512,1024]{1,0:T(8,128)(2,1)}, bf16[512,1024]{1,0:T(8,128)(2,1)S(1)}, u32[]{:S(2)}, u32[]{:S(2)}) collective-permute-start(bf16[512,1024]{1,0:T(8,128)(2,1)} %param.30), channel_id=1, source_target_pairs={{0,28},{4,0},{8,4},{12,8},{16,12},{20,16},{24,20},{28,24},{1,29},{... | collective-permute-start | bytes 3145736 | tf_op jit(solution)/shard_map/ppermute | solution.py:18
  60.5 73.2 %collective-permute-start.1 = (bf16[1024,1024]{1,0:T(8,128)(2,1)}, bf16[1024,1024]{1,0:T(8,128)(2,1)}, u32[]{:S(2)}, u32[]{:S(2)}) collective-permute-start(bf16[1024,1024]{1,0:T(8,128)(2,1)} %pad_maximum_fusion.2), channel_id=1, source_target_pairs={{0,24},{4,28},{8,0},{12,4},{16,8},{20,12},{24,16},{28,20},{1,25},{... | collective-permute-start | bytes 6291464 | tf_op jit(solution)/shard_map/ppermute | solution.py:18
  60.5 968.0 %all-gather.21.cloned.1.call-start = ((), (), s32[]{:S(2)}) async-start(), calls=%async_computation.13 | async-start | bytes 9437184 | tf_op jit(solution)/shard_map/all_gather | solution.py:239
  60.6 70.9 %collective-permute-start.3 = (bf16[512,1024]{1,0:T(8,128)(2,1)S(1)}, bf16[512,1024]{1,0:T(8,128)(2,1)S(1)}, u32[]{:S(2)}, u32[]{:S(2)}) collective-permute-start(bf16[512,1024]{1,0:T(8,128)(2,1)S(1)} %copy-done.17), channel_id=1, source_target_pairs={{0,28},{4,0},{8,4},{12,8},{16,12},{20,16},{24,20},{28,24},{1,29},{... | collective-permute-start | bytes 3145736 | tf_op jit(solution)/shard_map/ppermute | solution.py:18
  133.1 95.2 %collective-permute-start.4 = (bf16[1024,1024]{1,0:T(8,128)(2,1)}, bf16[1024,1024]{1,0:T(8,128)(2,1)}, u32[]{:S(2)}, u32[]{:S(2)}) collective-permute-start(bf16[1024,1024]{1,0:T(8,128)(2,1)} %pad_maximum_fusion.3), channel_id=1, source_target_pairs={{0,24},{4,28},{8,0},{12,4},{16,8},{20,12},{24,16},{28,20},{1,25},{... | collective-permute-start | bytes 6291464 | tf_op jit(solution)/shard_map/ppermute | solution.py:18
  137.1 531.1 %collective-permute-start.2 = (bf16[2048,1024]{1,0:T(8,128)(2,1)}, bf16[2048,1024]{1,0:T(8,128)(2,1)}, u32[]{:S(2)}, u32[]{:S(2)}) collective-permute-start(bf16[2048,1024]{1,0:T(8,128)(2,1)} %pad_maximum_fusion), channel_id=1, source_target_pairs={{0,16},{4,20},{8,24},{12,28},{16,0},{20,4},{24,8},{28,12},{1,17},{... | collective-permute-start | bytes 12582920 | tf_op jit(solution)/shard_map/ppermute | solution.py:18
  139.1 1033.6 %reduce-scatter.11.cloned.1.call-start = ((), (), s32[]{:S(2)}) async-start(), calls=%async_computation.15 | async-start | bytes 2359296 | tf_op jit(solution)/shard_map/reduce_scatter | solution.py:253
  231.9 471.5 %collective-permute-start.5 = (bf16[2048,1024]{1,0:T(8,128)(2,1)}, bf16[2048,1024]{1,0:T(8,128)(2,1)}, u32[]{:S(2)}, u32[]{:S(2)}) collective-permute-start(bf16[2048,1024]{1,0:T(8,128)(2,1)} %pad_maximum_fusion.1), channel_id=1, source_target_pairs={{0,16},{4,20},{8,24},{12,28},{16,0},{20,4},{24,8},{28,12},{1,17},{... | collective-permute-start | bytes 12582920 | tf_op jit(solution)/shard_map/ppermute | solution.py:18
  1097.3 138.3 %reduce-scatter.19.cloned.1.call-start = ((), (), s32[]{:S(2)}) async-start(), calls=%async_computation.19 | async-start | bytes 2359296 | tf_op jit(solution)/shard_map/reduce_scatter | solution.py:253
  1122.5 233.7 %reduce-scatter.9.cloned.1.call-start = ((), (), s32[]{:S(2)}) async-start(), calls=%async_computation.14 | async-start | bytes 7077888 | tf_op jit(solution)/shard_map/reduce_scatter | solution.py:250
  1136.4 340.5 %reduce-scatter.17.cloned.1.call-start = ((), (), s32[]{:S(2)}) async-start(), calls=%async_computation.18 | async-start | bytes 7077888 | tf_op jit(solution)/shard_map/reduce_scatter | solution.py:250
  1141.9 485.4 %reduce-scatter.13.cloned.1.call-start = ((), (), s32[]{:S(2)}) async-start(), calls=%async_computation.16 | async-start | bytes 9437184 | tf_op jit(solution)/shard_map/reduce_scatter | solution.py:259
  1149.9 627.5 %reduce-scatter.15.cloned.1.call-start = ((), (), s32[]{:S(2)}) async-start(), calls=%async_computation.17 | async-start | bytes 9437184 | tf_op jit(solution)/shard_map/reduce_scatter | solution.py:262
  1159.5 768.1 %reduce-scatter.21.cloned.1.call-start = ((), (), s32[]{:S(2)}) async-start(), calls=%async_computation.20 | async-start | bytes 9437184 | tf_op jit(solution)/shard_map/reduce_scatter | solution.py:259
  1166.2 911.5 %reduce-scatter.23.cloned.1.call-start = ((), (), s32[]{:S(2)}) async-start(), calls=%async_computation.21 | async-start | bytes 9437184 | tf_op jit(solution)/shard_map/reduce_scatter | solution.py:262
  1172.5 906.4 %copy-start.29 = (f32[256,1024]{1,0:T(8,128)S(1)}, f32[256,1024]{1,0:T(8,128)}, u32[]{:S(2)}) copy-start(f32[256,1024]{1,0:T(8,128)} %copy-done.28) | copy-start | bytes 3145732
  1172.5 906.4 %copy-start.36 = (f32[32,1024]{1,0:T(8,128)S(1)}, f32[32,1024]{1,0:T(8,128)}, u32[]{:S(2)}) copy-start(f32[32,1024]{1,0:T(8,128)} %convolution_add_fusion.2) | copy-start | bytes 393220
  1172.5 907.9 %copy-start.63 = (f32[256]{0:T(256)S(1)}, f32[256]{0:T(256)}, u32[]{:S(2)}) copy-start(f32[256]{0:T(256)} %copy-done.61) | copy-start | bytes 3076
  1172.5 1028.0 %all-reduce.9.cloned.1.call-start = ((), (), s32[]{:S(2)}) async-start(), calls=%async_computation.22 | async-start | bytes 12582912 | tf_op jit(solution)/shard_map/psum | solution.py:268
  (92 other events, 6507.2 us)
Sparse Core Ops, SparseCore 0:
  10.2 300.2 all-gather.10
  312.6 317.3 all-gather.12
  632.2 123.0 all-gather.14
  757.3 96.8 all-gather.16
  856.2 47.3 all-gather.18
  905.5 122.9 all-gather.20
  1097.4 66.6 reduce-scatter.10
  1168.1 67.3 reduce-scatter.18
  1239.1 116.9 reduce-scatter.8
  1359.6 117.2 reduce-scatter.16
  1480.5 146.7 reduce-scatter.12
  1630.8 146.5 reduce-scatter.14
  1781.0 146.5 reduce-scatter.20
  1931.1 146.5 reduce-scatter.22
  2080.4 120.1 all-reduce.8
